TPU v7x, 32 devices: a whole 2x2x4 slice. The times are simulated.
32 devices in a mesh: groups: 2 (over y), row: 8 (over z, x), col: 2 (over core).
Axes of the slice: x: 2, y: 2, z: 4, core: 2. Of those that a mesh axis runs over, the one named last changes fastest.
Arguments:
- inputs: bfloat16 [32, 8192], P(('groups', 'row'), 'col'), parts along dimension 0, may hold values from -6 to 6
- out_grads: bfloat16 [32, 8192], P(('groups', 'row'), 'col'), parts along dimension 0, may hold values from -6 to 6
- w_gate: bfloat16 [8192, 24576], P('col', 'row'), may hold values from -0.0625 to 0.0625
- w_up: bfloat16 [8192, 24576], P('col', 'row'), may hold values from -0.0625 to 0.0625
- w_down: bfloat16 [24576, 8192], P('row', 'col'), may hold values from -0.0390625 to 0.0390625
Outputs:
- attribution: float32 [32, 8192], P(('groups', 'row'), 'col'), parts along dimension 0
There are 2 independent parts, one for each index of `groups`. A program takes and returns all parts, laid end to end along the dimension named above; an argument that names none is the same for every part. Nothing has to cross between parts.
All inputs are finite; a program needn't handle non-finite values.
Results may differ from a plain program's by a relative error of at most 0.0029.
Values may be sent and summed in bfloat16 or wider, within the bound.
A program may use at most 192 MiB of HBM per device.

v0:
```python
import jax
import jax.numpy as jnp
from jax import lax
from jax.sharding import PartitionSpec as P


def derivatives(sums):
    gated = sums[0]
    upward = sums[1]
    backward = sums[2]
    sigma = jax.nn.sigmoid(gated)
    grad_gate = (backward * upward * sigma * (1.0 + gated * (1.0 - sigma))).astype(jnp.bfloat16)
    grad_up = (backward * gated * sigma).astype(jnp.bfloat16)
    return jnp.stack([grad_gate, grad_up])


def per_device(inputs, out_grads, w_gate, w_up, w_down):
    stacked = jnp.stack([inputs, out_grads])
    piece = lax.all_gather(stacked, "row", axis=1, tiled=True)
    gated = jnp.dot(piece[0], w_gate, preferred_element_type=jnp.float32)
    upward = jnp.dot(piece[0], w_up, preferred_element_type=jnp.float32)
    backward = lax.dot_general(
        piece[1], w_down, (((1,), (1,)), ((), ())), preferred_element_type=jnp.float32
    )
    partial_sums = jnp.stack([gated, upward, backward])
    summed = lax.psum(partial_sums, "col")
    derived = derivatives(summed)
    total = lax.dot_general(
        derived[0], w_gate, (((1,), (1,)), ((), ())), preferred_element_type=jnp.float32
    )
    grad_input = lax.psum_scatter(
        total
        + lax.dot_general(
            derived[1], w_up, (((1,), (1,)), ((), ())), preferred_element_type=jnp.float32
        ),
        "row",
        scatter_dimension=0,
        tiled=True,
    )
    return inputs.astype(jnp.float32) * grad_input


def solution(mesh):
    in_specs = (
        P(("groups", "row"), "col"),
        P(("groups", "row"), "col"),
        P("col", "row"),
        P("col", "row"),
        P("row", "col"),
    )
    out_specs = P(("groups", "row"), "col")
    return jax.shard_map(
        per_device, mesh=mesh, in_specs=in_specs, out_specs=out_specs, check_vma=False
    )
```

profile of v0, /device:TPU:0, one launch (start us, length us, event | category | flops | bytes accessed | tf_op | source)
XLA Modules:
  0.0 200.1 jit_solution(14004625171131348486)
XLA Ops:
  6.5 0.0 all-reduce.4.cloned.1.call-start
  6.5 0.8 pad_maximum_fusion.1
  7.4 32.5 %all_gather.3 = bf16[2,16,4096]{2,0,1:T(2,128)(2,1)S(1)} all-gather(bf16[2,2,4096]{2,0,1:T(2,128)(2,1)S(1)} %copy.6), channel_id=1, replica_groups=mesh['groups'=2,'row'=8,'col'=2] {'row'}, dimensions={1}, use_global_device_ids=true | all-gather | bytes 294912 | tf_op jit(solution)/shard_map/all_gather | solution.py:19
  39.9 0.4 fusion.10
  40.3 10.0 %convolution_bitcast_fusion.1 = f32[1,16,3072]{2,1,0:T(8,128)S(1)} fusion(bf16[4096,3072]{1,0:T(8,128)(2,1)} %param.8, bf16[1,16,4096]{2,0,1:T(2,128)(2,1)S(1)} %get-tuple-element.5), kind=kOutput, calls=%fused_computation.2 | convolution fusion | flops 402653184 | bytes 25493504 | tf_op jit(solution)/shard_map/dot_general | solution.py:21
  50.2 10.0 %convolution_bitcast_fusion.2 = f32[1,16,3072]{2,1,0:T(8,128)S(1)} fusion(bf16[4096,3072]{1,0:T(8,128)(2,1)} %param.7, bf16[1,16,4096]{2,0,1:T(2,128)(2,1)S(1)} %get-tuple-element.5), kind=kOutput, calls=%fused_computation.3 | convolution fusion | flops 402653184 | bytes 25493504 | tf_op jit(solution)/shard_map/dot_general | solution.py:20
  60.2 11.5 %convolution_bitcast_fusion = f32[1,16,3072]{2,1,0:T(8,128)S(1)} fusion(bf16[3072,4096]{1,0:T(8,128)(2,1)} %param.9, bf16[1,16,4096]{2,0,1:T(2,128)(2,1)S(1)} %get-tuple-element.6), kind=kOutput, calls=%fused_computation.1 | convolution fusion | flops 402653184 | bytes 25493504 | tf_op jit(solution)/shard_map/dot_general | solution.py:22
  71.7 0.9 pad_maximum_fusion
  72.6 0.0 all-reduce.4.cloned.1.call-update
  72.6 0.0 all-reduce.6.cloned.1.call-start
  72.7 19.9 %all-reduce.4.cloned.1.call-done = f32[3,16,3072]{2,1,0:T(8,128)} async-done(((f32[3,16,3072]{2,1,0:T(8,128)}), f32[3,16,3072]{2,1,0:T(8,128)}) %all-reduce.4.cloned.1.call-update) | async-done | bytes 589840 | tf_op jit(solution)/shard_map/psum | solution.py:26
  92.6 0.0 copy-start
  92.6 14.9 %fusion.4 = f32[16,4096]{1,0:T(8,128)S(1)} fusion(bf16[4096,3072]{1,0:T(8,128)(2,1)} %param.7, f32[3,16,3072]{2,1,0:T(8,128)} %all-reduce.4.cloned.1.call-done), kind=kOutput, calls=%fused_computation.16 | convolution fusion | flops 403144704 | bytes 26017792 | tf_op jit(solution)/shard_map/dot_general | solution.py:28
  107.5 0.0 copy-done
  107.5 0.0 copy-start.2
  107.5 0.0 copy-start.1
  107.5 12.3 %convolution_add_fusion = f32[16,4096]{1,0:T(8,128)} fusion(f32[16,4096]{1,0:T(8,128)S(1)} %fusion.4, bf16[4096,3072]{1,0:T(8,128)(2,1)} %param.8, f32[3,16,3072]{2,1,0:T(8,128)S(1)} %copy-done), kind=kOutput, calls=%fused_computation | convolution fusion | flops 403013632 | bytes 26083328 | tf_op jit(solution)/shard_map/dot_general | solution.py:33
  119.8 0.0 all-reduce.6.cloned.1.call-update
  119.8 0.0 copy-done.2
  119.8 0.6 dynamic-slice
  121.1 70.6 %all-reduce.6.cloned.1.call-done = f32[16,4096]{1,0:T(8,128)} async-done(((f32[16,4096]{1,0:T(8,128)}), f32[16,4096]{1,0:T(8,128)}) %all-reduce.6.cloned.1.call-update) | async-done | bytes 262160
  191.7 0.0 copy-done.1
  191.7 1.5 dynamic-slice_multiply_fusion
  (1 shorter events, 0.0 us)
Async XLA Ops:
  6.5 86.1 %all-reduce.4.cloned.1.call-start = ((), (), s32[]{:S(2)}) async-start(), calls=%async_computation | async-start | bytes 1179648 | tf_op jit(solution)/shard_map/psum | solution.py:26
  72.6 119.1 %all-reduce.6.cloned.1.call-start = ((), (), s32[]{:S(2)}) async-start(), calls=%async_computation.1 | async-start | bytes 524288
  92.6 14.9 %copy-start = (f32[3,16,3072]{2,1,0:T(8,128)S(1)}, f32[3,16,3072]{2,1,0:T(8,128)}, u32[]{:S(2)}) copy-start(f32[3,16,3072]{2,1,0:T(8,128)} %all-reduce.4.cloned.1.call-done) | copy-start | bytes 1769476
  107.5 12.3 %copy-start.2 = (u32[32]{0:T(128)S(1)}, u32[32]{0:T(128)}, u32[]{:S(2)}) copy-start(u32[32]{0:T(128)} %constant.6) | copy-start | bytes 388
  107.5 84.2 %copy-start.1 = (bf16[2,4096]{1,0:T(2,128)(2,1)S(1)}, bf16[2,4096]{1,0:T(2,128)(2,1)}, u32[]{:S(2)}) copy-start(bf16[2,4096]{1,0:T(2,128)(2,1)} %param.5) | copy-start | bytes 49156
Sparse Core Ops, SparseCore 0:
  72.8 19.7 all-reduce.3
  119.9 71.7 all-reduce.5
where the time goes:
time: 200 us
  waiting for transfers between devices  90.6 us (45%)
  matrix products  58.6 us (29%)
  blocking collectives  32.5 us (16%)
  between operations  14.1 us (7%)
  other arithmetic  3.21 us (2%)
    unnamed x3, waiting for transfers between devices  70.7 us
    all_gather x1, blocking collectives, per_device(): piece = lax.all_gather(stacked, 'row', axis=1, tiled=True)  32.5 us
    psum x1, waiting for transfers between devices, per_device(): summed = lax.psum(partial_sums, 'col')  19.9 us
    dot_general x1, matrix products, per_device(): lax.dot_general(derived[0], w_gate, (((1,), (1,)), ((), ())), preferred_e...  14.9 us
    dot_general x1, matrix products, per_device(): lax.dot_general(derived[1], w_up, (((1,), (1,)), ((), ())), preferred_ele...  12.3 us
    dot_general x1, matrix products, per_device(): lax.dot_general(piece[1], w_down, (((1,), (1,)), ((), ())), preferred_ele...  11.5 us
    dot_general x1, matrix products, per_device(): gated = jnp.dot(piece[0], w_gate, preferred_element_type=jnp.float32)  9.97 us
    dot_general x1, matrix products, per_device(): upward = jnp.dot(piece[0], w_up, preferred_element_type=jnp.float32)  9.97 us
  transfers between devices with their start and end apart: 2, of which 2 were waited for; matrix products, arithmetic and copies ran while one was open for 0% of the time, Pallas kernels for 0%

commit v1 on v0

--- a/solution.py
+++ b/solution.py
@@ -16,7 +16,14 @@
 
 def per_device(inputs, out_grads, w_gate, w_up, w_down):
     stacked = jnp.stack([inputs, out_grads])
-    piece = lax.all_gather(stacked, "row", axis=1, tiled=True)
+    view_out, y = (lax.axis_size("row"), lax.axis_index("row"))
+    piece, met_up = (stacked, 1)
+    while met_up < view_out:
+        carry_out = lax.ppermute(piece, "row", tuple(((i, i ^ met_up) for i in range(view_out))))
+        r_now = jnp.concatenate([piece, carry_out], axis=1)
+        prior = jnp.concatenate([carry_out, piece], axis=1)
+        piece = jnp.where(y & met_up == 0, r_now, prior)
+        met_up = 2 * met_up
     gated = jnp.dot(piece[0], w_gate, preferred_element_type=jnp.float32)
     upward = jnp.dot(piece[0], w_up, preferred_element_type=jnp.float32)
     backward = lax.dot_general(

time: 200 us -> 186 us (0.930)
  blocking collectives: 32.5 us -> 0 us
  waiting for transfers between devices: 90.6 us -> 99.6 us
  starting transfers between devices: 0.04 us -> 8.32 us
    all_gather x1 -> x0, blocking collectives: 32.5 us -> none  [per_device(): piece = lax.all_gather(stacked, 'row', axis=1, tiled=True)]
    ppermute x0 -> x3, starting transfers between devices: none -> 8.27 us  [per_device(): lax.ppermute(piece, 'row', tuple(((i, i ^ met_up) for i in range(view_out...]
    ppermute x0 -> x3, waiting for transfers between devices: none -> 7.1 us  [per_device(): lax.ppermute(piece, 'row', tuple(((i, i ^ met_up) for i in range(view_out...]
  transfers between devices with their start and end apart: 2 -> 5, of which waited for: 2 -> 5; matrix products, arithmetic and copies ran while one was open for 0% -> 0% of each run, Pallas kernels for 0% -> 0%
where the time goes in v1:
time: 186 us; the launch traced here: 185 us
  waiting for transfers between devices  99.6 us (54%)
  matrix products  58.4 us (31%)
  between operations  14.1 us (8%)
  starting transfers between devices  8.32 us (4%)
  other arithmetic  4.3 us (2%)
    unnamed x3, waiting for transfers between devices  70.7 us
    psum x1, waiting for transfers between devices, per_device(): summed = lax.psum(partial_sums, 'col')  21.8 us
    dot_general x1, matrix products, per_device(): lax.dot_general(derived[0], w_gate, (((1,), (1,)), ((), ())), preferred_e...  14.9 us
    dot_general x1, matrix products, per_device(): lax.dot_general(derived[1], w_up, (((1,), (1,)), ((), ())), preferred_ele...  12.3 us
    dot_general x1, matrix products, per_device(): lax.dot_general(piece[1], w_down, (((1,), (1,)), ((), ())), preferred_ele...  11.5 us
    dot_general x1, matrix products, per_device(): upward = jnp.dot(piece[0], w_up, preferred_element_type=jnp.float32)  9.89 us
    dot_general x1, matrix products, per_device(): gated = jnp.dot(piece[0], w_gate, preferred_element_type=jnp.float32)  9.89 us
    ppermute x3, starting transfers between devices, per_device(): lax.ppermute(piece, 'row', tuple(((i, i ^ met_up) for i in range(view_out...  8.27 us
  transfers between devices with their start and end apart: 5, of which 5 were waited for; matrix products, arithmetic and copies ran while one was open for 0% of the time, Pallas kernels for 0%

profile of v1, /device:TPU:0, one launch (start us, length us, event | category | flops | bytes accessed | tf_op | source)
XLA Modules:
  0.0 185.3 jit_solution(4549336296371238831)
XLA Ops:
  6.5 0.0 all-reduce.4.cloned.1.call-start
  6.5 0.8 pad_maximum_fusion.1
  7.3 3.0 %collective-permute-start = (bf16[2,2,4096]{2,1,0:T(2,128)(2,1)S(1)}, bf16[2,2,4096]{2,1,0:T(2,128)(2,1)S(1)}, u32[]{:S(2)}, u32[]{:S(2)}) collective-permute-start(bf16[2,2,4096]{2,1,0:T(2,128)(2,1)S(1)} %pad_maximum_fusion.1), channel_id=1, source_target_pairs={{0,2},{2,0},{4,6},{6,4},{8,10},{10,8},{12,14},{14,12},{1,3},{3,1},... | collective-permute-start | bytes 98312 | tf_op jit(solution)/shard_map/ppermute | solution.py:22
  10.3 1.9 %collective-permute-done = bf16[2,2,4096]{2,1,0:T(2,128)(2,1)S(1)} collective-permute-done((bf16[2,2,4096]{2,1,0:T(2,128)(2,1)S(1)}, bf16[2,2,4096]{2,1,0:T(2,128)(2,1)S(1)}, u32[]{:S(2)}, u32[]{:S(2)}) %collective-permute-start) | collective-permute-done | bytes 32800 | tf_op jit(solution)/shard_map/ppermute | solution.py:22
  12.2 0.9 maximum_select_fusion.2
  13.2 2.2 %collective-permute-start.1 = (bf16[2,4,4096]{2,1,0:T(4,128)(2,1)S(1)}, bf16[2,4,4096]{2,1,0:T(4,128)(2,1)S(1)}, u32[]{:S(2)}, u32[]{:S(2)}) collective-permute-start(bf16[2,4,4096]{2,1,0:T(4,128)(2,1)S(1)} %maximum_select_fusion.2), channel_id=1, source_target_pairs={{0,4},{2,6},{4,0},{6,2},{8,12},{10,14},{12,8},{14,10},{1,5},{3,7},... | collective-permute-start | bytes 196616 | tf_op jit(solution)/shard_map/ppermute | solution.py:22
  15.3 2.2 %collective-permute-done.1 = bf16[2,4,4096]{2,1,0:T(4,128)(2,1)S(1)} collective-permute-done((bf16[2,4,4096]{2,1,0:T(4,128)(2,1)S(1)}, bf16[2,4,4096]{2,1,0:T(4,128)(2,1)S(1)}, u32[]{:S(2)}, u32[]{:S(2)}) %collective-permute-start.1) | collective-permute-done | bytes 65568 | tf_op jit(solution)/shard_map/ppermute | solution.py:22
  17.6 0.1 maximum_select_fusion.1
  17.7 3.1 %collective-permute-start.2 = (bf16[2,8,4096]{2,1,0:T(8,128)(2,1)S(1)}, bf16[2,8,4096]{2,1,0:T(8,128)(2,1)S(1)}, u32[]{:S(2)}, u32[]{:S(2)}) collective-permute-start(bf16[2,8,4096]{2,1,0:T(8,128)(2,1)S(1)} %maximum_select_fusion.1), channel_id=1, source_target_pairs={{0,8},{2,10},{4,12},{6,14},{8,0},{10,2},{12,4},{14,6},{1,9},{3,11}... | collective-permute-start | bytes 393224 | tf_op jit(solution)/shard_map/ppermute | solution.py:22
  20.8 3.0 %collective-permute-done.2 = bf16[2,8,4096]{2,1,0:T(8,128)(2,1)S(1)} collective-permute-done((bf16[2,8,4096]{2,1,0:T(8,128)(2,1)S(1)}, bf16[2,8,4096]{2,1,0:T(8,128)(2,1)S(1)}, u32[]{:S(2)}, u32[]{:S(2)}) %collective-permute-start.2) | collective-permute-done | bytes 131104 | tf_op jit(solution)/shard_map/ppermute | solution.py:22
  23.8 11.5 %convolution_bitcast_fusion = f32[1,16,3072]{2,1,0:T(8,128)S(1)} fusion(bf16[3072,4096]{1,0:T(8,128)(2,1)} %param.9, bf16[2,16,4096]{2,1,0:T(8,128)(2,1)S(1)} %maximum_select_fusion), kind=kOutput, calls=%fused_computation.1 | convolution fusion | flops 402653184 | bytes 25493504 | tf_op jit(solution)/shard_map/dot_general | solution.py:29
  35.3 9.9 %convolution_bitcast_fusion.1 = f32[1,16,3072]{2,1,0:T(8,128)S(1)} fusion(bf16[4096,3072]{1,0:T(8,128)(2,1)} %param.8, bf16[2,16,4096]{2,1,0:T(8,128)(2,1)S(1)} %maximum_select_fusion), kind=kOutput, calls=%fused_computation.2 | convolution fusion | flops 402653184 | bytes 25493504 | tf_op jit(solution)/shard_map/dot_general | solution.py:28
  45.2 9.9 %convolution_bitcast_fusion.2 = f32[1,16,3072]{2,1,0:T(8,128)S(1)} fusion(bf16[4096,3072]{1,0:T(8,128)(2,1)} %param.7, bf16[2,16,4096]{2,1,0:T(8,128)(2,1)S(1)} %maximum_select_fusion), kind=kOutput, calls=%fused_computation.3 | convolution fusion | flops 402653184 | bytes 25493504 | tf_op jit(solution)/shard_map/dot_general | solution.py:27
  55.1 0.9 pad_maximum_fusion
  56.0 0.0 all-reduce.4.cloned.1.call-update
  56.0 0.0 all-reduce.6.cloned.1.call-start
  56.1 21.8 %all-reduce.4.cloned.1.call-done = f32[3,16,3072]{2,1,0:T(8,128)} async-done(((f32[3,16,3072]{2,1,0:T(8,128)}), f32[3,16,3072]{2,1,0:T(8,128)}) %all-reduce.4.cloned.1.call-update) | async-done | bytes 589840 | tf_op jit(solution)/shard_map/psum | solution.py:33
  77.9 0.0 copy-start
  77.9 14.9 %fusion.4 = f32[16,4096]{1,0:T(8,128)S(1)} fusion(bf16[4096,3072]{1,0:T(8,128)(2,1)} %param.7, f32[3,16,3072]{2,1,0:T(8,128)} %all-reduce.4.cloned.1.call-done), kind=kOutput, calls=%fused_computation.18 | convolution fusion | flops 403144704 | bytes 26017792 | tf_op jit(solution)/shard_map/dot_general | solution.py:35
  92.8 0.0 copy-done
  92.8 0.0 copy-start.2
  92.8 0.0 copy-start.1
  92.8 12.3 %convolution_add_fusion = f32[16,4096]{1,0:T(8,128)} fusion(f32[16,4096]{1,0:T(8,128)S(1)} %fusion.4, bf16[4096,3072]{1,0:T(8,128)(2,1)} %param.8, f32[3,16,3072]{2,1,0:T(8,128)S(1)} %copy-done), kind=kOutput, calls=%fused_computation | convolution fusion | flops 403013632 | bytes 26083328 | tf_op jit(solution)/shard_map/dot_general | solution.py:40
  105.0 0.0 all-reduce.6.cloned.1.call-update
  105.1 0.0 copy-done.2
  105.1 0.6 dynamic-slice
  106.3 70.6 %all-reduce.6.cloned.1.call-done = f32[16,4096]{1,0:T(8,128)} async-done(((f32[16,4096]{1,0:T(8,128)}), f32[16,4096]{1,0:T(8,128)}) %all-reduce.6.cloned.1.call-update) | async-done | bytes 262160
  177.0 0.0 copy-done.1
  177.0 1.5 dynamic-slice_multiply_fusion
  (1 shorter events, 0.0 us)
Async XLA Ops:
  6.5 71.3 %all-reduce.4.cloned.1.call-start = ((), (), s32[]{:S(2)}) async-start(), calls=%async_computation | async-start | bytes 1179648 | tf_op jit(solution)/shard_map/psum | solution.py:33
  7.3 4.9 %collective-permute-start = (bf16[2,2,4096]{2,1,0:T(2,128)(2,1)S(1)}, bf16[2,2,4096]{2,1,0:T(2,128)(2,1)S(1)}, u32[]{:S(2)}, u32[]{:S(2)}) collective-permute-start(bf16[2,2,4096]{2,1,0:T(2,128)(2,1)S(1)} %pad_maximum_fusion.1), channel_id=1, source_target_pairs={{0,2},{2,0},{4,6},{6,4},{8,10},{10,8},{12,14},{14,12},{1,3},{3,1},... | collective-permute-start | bytes 98312 | tf_op jit(solution)/shard_map/ppermute | solution.py:22
  13.2 4.4 %collective-permute-start.1 = (bf16[2,4,4096]{2,1,0:T(4,128)(2,1)S(1)}, bf16[2,4,4096]{2,1,0:T(4,128)(2,1)S(1)}, u32[]{:S(2)}, u32[]{:S(2)}) collective-permute-start(bf16[2,4,4096]{2,1,0:T(4,128)(2,1)S(1)} %maximum_select_fusion.2), channel_id=1, source_target_pairs={{0,4},{2,6},{4,0},{6,2},{8,12},{10,14},{12,8},{14,10},{1,5},{3,7},... | collective-permute-start | bytes 196616 | tf_op jit(solution)/shard_map/ppermute | solution.py:22
  17.7 6.1 %collective-permute-start.2 = (bf16[2,8,4096]{2,1,0:T(8,128)(2,1)S(1)}, bf16[2,8,4096]{2,1,0:T(8,128)(2,1)S(1)}, u32[]{:S(2)}, u32[]{:S(2)}) collective-permute-start(bf16[2,8,4096]{2,1,0:T(8,128)(2,1)S(1)} %maximum_select_fusion.1), channel_id=1, source_target_pairs={{0,8},{2,10},{4,12},{6,14},{8,0},{10,2},{12,4},{14,6},{1,9},{3,11}... | collective-permute-start | bytes 393224 | tf_op jit(solution)/shard_map/ppermute | solution.py:22
  56.0 121.0 %all-reduce.6.cloned.1.call-start = ((), (), s32[]{:S(2)}) async-start(), calls=%async_computation.1 | async-start | bytes 524288
  77.9 14.9 %copy-start = (f32[3,16,3072]{2,1,0:T(8,128)S(1)}, f32[3,16,3072]{2,1,0:T(8,128)}, u32[]{:S(2)}) copy-start(f32[3,16,3072]{2,1,0:T(8,128)} %all-reduce.4.cloned.1.call-done) | copy-start | bytes 1769476
  92.8 12.3 %copy-start.2 = (u32[32]{0:T(128)S(1)}, u32[32]{0:T(128)}, u32[]{:S(2)}) copy-start(u32[32]{0:T(128)} %constant.20) | copy-start | bytes 388
  92.8 84.2 %copy-start.1 = (bf16[2,4096]{1,0:T(2,128)(2,1)S(1)}, bf16[2,4096]{1,0:T(2,128)(2,1)}, u32[]{:S(2)}) copy-start(bf16[2,4096]{1,0:T(2,128)(2,1)} %param.5) | copy-start | bytes 49156
Sparse Core Ops, SparseCore 0:
  56.1 21.6 all-reduce.3
  105.2 71.7 all-reduce.5

commit v2 on v0

--- a/solution.py
+++ b/solution.py
@@ -23,7 +23,8 @@
         piece[1], w_down, (((1,), (1,)), ((), ())), preferred_element_type=jnp.float32
     )
     partial_sums = jnp.stack([gated, upward, backward])
-    summed = lax.psum(partial_sums, "col")
+    parts = lax.all_gather(partial_sums, "col")
+    summed = jnp.sum(parts, axis=0)
     derived = derivatives(summed)
     total = lax.dot_general(
         derived[0], w_gate, (((1,), (1,)), ((), ())), preferred_element_type=jnp.float32

time: 200 us -> 189 us (0.945)
  waiting for transfers between devices: 90.6 us -> 81 us
  matrix products: 58.6 us -> 55.2 us
    psum x1 -> x0, waiting for transfers between devices: 19.9 us -> none  [per_device(): summed = lax.psum(partial_sums, 'col')]
    all_gather x0 -> x1, waiting for transfers between devices: none -> 10.3 us  [per_device(): parts = lax.all_gather(partial_sums, 'col')]
    dot_general x1, matrix products: 14.9 us -> 11.5 us  [per_device(): lax.dot_general(derived[0], w_gate, (((1,), (1,)), ((), ())), preferred_e...]
where the time goes in v2:
time: 189 us
  waiting for transfers between devices  81 us (43%)
  matrix products  55.2 us (29%)
  blocking collectives  32.5 us (17%)
  between operations  14.1 us (7%)
  other arithmetic  4.63 us (2%)
    unnamed x3, waiting for transfers between devices  70.7 us
    all_gather x1, blocking collectives, per_device(): piece = lax.all_gather(stacked, 'row', axis=1, tiled=True)  32.5 us
    dot_general x1, matrix products, per_device(): lax.dot_general(derived[1], w_up, (((1,), (1,)), ((), ())), preferred_ele...  12.3 us
    dot_general x1, matrix products, per_device(): lax.dot_general(piece[1], w_down, (((1,), (1,)), ((), ())), preferred_ele...  11.5 us
    dot_general x1, matrix products, per_device(): lax.dot_general(derived[0], w_gate, (((1,), (1,)), ((), ())), preferred_e...  11.5 us
    all_gather x1, waiting for transfers between devices, per_device(): parts = lax.all_gather(partial_sums, 'col')  10.3 us
    dot_general x1, matrix products, per_device(): gated = jnp.dot(piece[0], w_gate, preferred_element_type=jnp.float32)  9.97 us
    dot_general x1, matrix products, per_device(): upward = jnp.dot(piece[0], w_up, preferred_element_type=jnp.float32)  9.97 us
  transfers between devices with their start and end apart: 2, of which 2 were waited for; matrix products, arithmetic and copies ran while one was open for 0% of the time, Pallas kernels for 0%

profile of v2, /device:TPU:0, one launch (start us, length us, event | category | flops | bytes accessed | tf_op | source)
XLA Modules:
  0.0 188.5 jit_solution(10522026716130323047)
XLA Ops:
  6.5 0.0 all-gather.3.cloned.1.call-start
  6.5 0.8 pad_maximum_fusion.1
  7.4 32.5 %all_gather.9 = bf16[2,16,4096]{2,0,1:T(2,128)(2,1)S(1)} all-gather(bf16[2,2,4096]{2,0,1:T(2,128)(2,1)S(1)} %copy.6), channel_id=1, replica_groups=mesh['groups'=2,'row'=8,'col'=2] {'row'}, dimensions={1}, use_global_device_ids=true | all-gather | bytes 294912 | tf_op jit(solution)/shard_map/all_gather | solution.py:19
  39.9 0.4 fusion.10
  40.3 10.0 %convolution_bitcast_fusion.1 = f32[1,16,3072]{2,1,0:T(8,128)S(1)} fusion(bf16[4096,3072]{1,0:T(8,128)(2,1)} %param.8, bf16[1,16,4096]{2,0,1:T(2,128)(2,1)S(1)} %get-tuple-element.5), kind=kOutput, calls=%fused_computation.2 | convolution fusion | flops 402653184 | bytes 25493504 | tf_op jit(solution)/shard_map/dot_general | solution.py:21
  50.2 10.0 %convolution_bitcast_fusion.2 = f32[1,16,3072]{2,1,0:T(8,128)S(1)} fusion(bf16[4096,3072]{1,0:T(8,128)(2,1)} %param.7, bf16[1,16,4096]{2,0,1:T(2,128)(2,1)S(1)} %get-tuple-element.5), kind=kOutput, calls=%fused_computation.3 | convolution fusion | flops 402653184 | bytes 25493504 | tf_op jit(solution)/shard_map/dot_general | solution.py:20
  60.2 11.5 %convolution_bitcast_fusion = f32[1,16,3072]{2,1,0:T(8,128)S(1)} fusion(bf16[3072,4096]{1,0:T(8,128)(2,1)} %param.9, bf16[1,16,4096]{2,0,1:T(2,128)(2,1)S(1)} %get-tuple-element.6), kind=kOutput, calls=%fused_computation.1 | convolution fusion | flops 402653184 | bytes 25493504 | tf_op jit(solution)/shard_map/dot_general | solution.py:22
  71.7 0.9 pad_maximum_fusion
  72.6 0.0 all-gather.3.cloned.1.call-update
  72.7 0.0 all-reduce.3.cloned.1.call-start
  72.7 10.3 %all-gather.3.cloned.1.call-done = f32[6,16,3072]{2,1,0:T(8,128)} async-done(((f32[3,16,3072]{2,1,0:T(8,128)}), f32[6,16,3072]{2,1,0:T(8,128)}) %all-gather.3.cloned.1.call-update) | async-done | bytes 1179664 | tf_op jit(solution)/shard_map/all_gather | solution.py:26
  83.0 1.4 reduce_sum.9
  84.4 11.5 %fusion.4 = f32[16,4096]{1,0:T(8,128)S(1)} fusion(bf16[4096,3072]{1,0:T(8,128)(2,1)} %param.7, f32[3,16,3072]{2,1,0:T(8,128)S(1)} %reduce_sum.9), kind=kOutput, calls=%fused_computation.16 | convolution fusion | flops 403144704 | bytes 26017792 | tf_op jit(solution)/shard_map/dot_general | solution.py:29
  95.9 0.0 copy-start.1
  95.9 0.0 copy-start
  95.9 12.3 %convolution_add_fusion = f32[16,4096]{1,0:T(8,128)} fusion(f32[16,4096]{1,0:T(8,128)S(1)} %fusion.4, bf16[4096,3072]{1,0:T(8,128)(2,1)} %param.8, f32[3,16,3072]{2,1,0:T(8,128)S(1)} %reduce_sum.9), kind=kOutput, calls=%fused_computation | convolution fusion | flops 403013632 | bytes 26083328 | tf_op jit(solution)/shard_map/dot_general | solution.py:34
  108.2 0.0 all-reduce.3.cloned.1.call-update
  108.2 0.0 copy-done.1
  108.2 0.6 dynamic-slice
  109.5 70.7 %all-reduce.3.cloned.1.call-done = f32[16,4096]{1,0:T(8,128)} async-done(((f32[16,4096]{1,0:T(8,128)}), f32[16,4096]{1,0:T(8,128)}) %all-reduce.3.cloned.1.call-update) | async-done | bytes 262160
  180.1 0.0 copy-done
  180.1 1.5 dynamic-slice_multiply_fusion
  (1 shorter events, 0.0 us)
Async XLA Ops:
  6.5 76.5 %all-gather.3.cloned.1.call-start = ((), (), s32[]{:S(2)}) async-start(), calls=%async_computation | async-start | bytes 1769472 | tf_op jit(solution)/shard_map/all_gather | solution.py:26
  72.7 107.5 %all-reduce.3.cloned.1.call-start = ((), (), s32[]{:S(2)}) async-start(), calls=%async_computation.1 | async-start | bytes 524288
  95.9 12.3 %copy-start.1 = (u32[32]{0:T(128)S(1)}, u32[32]{0:T(128)}, u32[]{:S(2)}) copy-start(u32[32]{0:T(128)} %constant.8) | copy-start | bytes 388
  95.9 84.2 %copy-start = (bf16[2,4096]{1,0:T(2,128)(2,1)S(1)}, bf16[2,4096]{1,0:T(2,128)(2,1)}, u32[]{:S(2)}) copy-start(bf16[2,4096]{1,0:T(2,128)(2,1)} %param.5) | copy-start | bytes 49156
Sparse Core Ops, SparseCore 0:
  72.8 10.1 all-gather.2
  108.3 71.7 all-reduce.2
